TPU v7x, 128 devices: a whole 4x4x4 slice. The times are simulated.
128 devices in a mesh: dp: 4 (over z), fsdp: 32 (over x, y, core).
Axes of the slice: x: 4, y: 4, z: 4, core: 2. Of those that a mesh axis runs over, the one named last changes fastest.
Arguments:
- tokens: bfloat16 [32768, 6144], P(('dp', 'fsdp')), may hold values from -6 to 6
- cotangent: bfloat16 [32768, 6144], P(('dp', 'fsdp')), may hold values from -6 to 6
- up_weight_blocks: bfloat16 [128, 128, 128], P('fsdp'), may hold values from -0.5 to 0.5
- down_weight_blocks: bfloat16 [128, 128, 128], P('fsdp'), may hold values from -0.5 to 0.5
- block_rows: int32 [128], replicated, may hold values from 0 to 47, as said below
- block_cols: int32 [128], replicated, may hold values from 0 to 191
- owner_counts: int32 [32], replicated, may hold values from 1 to 4, as said below
Outputs:
- output: bfloat16 [32768, 6144], P(('dp', 'fsdp'))
- input_grad: bfloat16 [32768, 6144], P(('dp', 'fsdp'))
- up_grad: float32 [128, 128, 128], P('fsdp')
- down_grad: float32 [128, 128, 128], P('fsdp')
Inputs may be any that keep to these rules, and one draw needn't show every extreme that they name: Owner o has owner_counts[o] live slots, its first ones; some owner has all 4 live. All 128 slots name distinct (block_rows, block_cols) pairs.
All inputs are finite; a program needn't handle non-finite values.
Results may differ from a plain program's by a relative error of at most 0.0049.
Values may be sent and summed in bfloat16 or wider, within the bound.
A program may use at most 256 MiB of HBM per device.

v0:
```python
import math
import jax
import jax.numpy as jnp
from jax import lax
from jax.sharding import PartitionSpec as P

D = 6144
FF = 24576
BLOCK_EDGE = 128
SLOTS = 4
gelu_scale = 0.7978845608028654
cubic_coef = 0.044715


def gelu_parts(values):
    inner_arg = gelu_scale * (values + cubic_coef * values * values * values)
    tanh_val = jnp.tanh(inner_arg)
    gelu_value = 0.5 * values * (1.0 + tanh_val)
    gelu_slope = 0.5 * (1.0 + tanh_val) + 0.5 * values * (
        1.0 - tanh_val * tanh_val
    ) * gelu_scale * (1.0 + 3.0 * cubic_coef * values * values)
    return (gelu_value, gelu_slope)


def to_blocks(source):
    token_count = source.shape[0]
    return source.reshape(token_count, source.shape[1] // BLOCK_EDGE, BLOCK_EDGE).transpose(1, 0, 2)


def from_blocks(blocks):
    return blocks.transpose(1, 0, 2).reshape(blocks.shape[1], blocks.shape[0] * BLOCK_EDGE)


def one_hot_table(index_list, width, dtype):
    return (index_list[:, None] == jnp.arange(width, dtype=jnp.int32)[None, :]).astype(dtype)


def pick_blocks(blocks, index_list):
    table = one_hot_table(index_list, blocks.shape[0], jnp.bfloat16)
    return jnp.einsum("sr,rnk->snk", table, blocks, preferred_element_type=jnp.float32).astype(
        jnp.bfloat16
    )


def spread_blocks(contrib, index_list, width):
    table = one_hot_table(index_list, width, jnp.float32)
    return jnp.einsum(
        "sc,snj->cnj",
        table,
        contrib,
        preferred_element_type=jnp.float32,
        precision=lax.Precision.HIGHEST,
    )


def on_device(
    tokens, cotangent, up_weight_blocks, down_weight_blocks, block_rows, block_cols, owner_counts
):
    token_count = tokens.shape[0]
    total_slots = block_rows.shape[0]
    row_blocks = D // BLOCK_EDGE
    col_blocks = FF // BLOCK_EDGE
    slot_position = jnp.arange(total_slots, dtype=jnp.int32)
    live_mask = slot_position % SLOTS < owner_counts[slot_position // SLOTS]
    x_blocks = to_blocks(tokens)
    dy_blocks = to_blocks(cotangent)

    def slot_info():
        return (block_rows, block_cols, live_mask.astype(jnp.bfloat16)[:, None, None])

    up_whole = lax.all_gather(up_weight_blocks, "fsdp", axis=0, tiled=True)
    row_ids, col_ids, keep_mask = slot_info()
    picked = pick_blocks(x_blocks, row_ids)
    contrib = jnp.einsum(
        "snk,skj->snj", picked, up_whole * keep_mask, preferred_element_type=jnp.float32
    )
    pre_act = spread_blocks(contrib, col_ids, col_blocks)
    gelu_value, gelu_slope = gelu_parts(pre_act)
    hidden = gelu_value.astype(jnp.bfloat16)
    row_ids, col_ids, keep_mask = slot_info()
    weights = lax.all_gather(down_weight_blocks, "fsdp", axis=0, tiled=True) * keep_mask
    h_pick = pick_blocks(hidden, col_ids)
    dy_pick = pick_blocks(dy_blocks, row_ids)
    out_part = jnp.einsum("snk,skj->snj", h_pick, weights, preferred_element_type=jnp.float32)
    back_part = jnp.einsum("snj,skj->snk", dy_pick, weights, preferred_element_type=jnp.float32)
    out_sum = spread_blocks(out_part, row_ids, row_blocks)
    hidden_grad = spread_blocks(back_part, col_ids, col_blocks)
    output = from_blocks(out_sum.astype(jnp.bfloat16))
    pre_grad = (hidden_grad * gelu_slope).astype(jnp.bfloat16)
    row_ids, col_ids, keep_mask = slot_info()
    picked = pick_blocks(pre_grad, col_ids)
    contrib = jnp.einsum(
        "snj,skj->snk", picked, up_whole * keep_mask, preferred_element_type=jnp.float32
    )
    in_sum = spread_blocks(contrib, row_ids, row_blocks)
    input_grad = from_blocks(in_sum.astype(jnp.bfloat16))
    dp_groups = lax.axis_size("dp")
    fsdp_owners = lax.axis_size("fsdp")
    grad_scale = 1.0 / math.sqrt(token_count * dp_groups * fsdp_owners)
    slot_list = jnp.arange(lax.axis_size("fsdp") * SLOTS, dtype=jnp.int32)
    keep_mask = live_mask[slot_list].astype(jnp.float32)[:, None, None]
    x_pick = pick_blocks(x_blocks, block_rows[slot_list])
    p_pick = pick_blocks(pre_grad, block_cols[slot_list])
    up_local = lax.psum_scatter(
        jnp.einsum("snk,snj->skj", x_pick, p_pick, preferred_element_type=jnp.float32) * keep_mask,
        "fsdp",
        scatter_dimension=0,
        tiled=True,
    )
    slot_list = jnp.arange(lax.axis_size("fsdp") * SLOTS, dtype=jnp.int32)
    keep_mask = live_mask[slot_list].astype(jnp.float32)[:, None, None]
    h_pick = pick_blocks(hidden, block_cols[slot_list])
    dy_pick = pick_blocks(dy_blocks, block_rows[slot_list])
    down_local = lax.psum_scatter(
        jnp.einsum("snk,snj->skj", h_pick, dy_pick, preferred_element_type=jnp.float32) * keep_mask,
        "fsdp",
        scatter_dimension=0,
        tiled=True,
    )
    up_grad, down_grad = lax.psum((up_local, down_local), "dp")
    return (output, input_grad, up_grad * grad_scale, down_grad * grad_scale)


def solution(mesh):
    in_specs = (
        P(("dp", "fsdp"), None),
        P(("dp", "fsdp"), None),
        P("fsdp", None, None),
        P("fsdp", None, None),
        P(),
        P(),
        P(),
    )
    out_specs = (
        P(("dp", "fsdp"), None),
        P(("dp", "fsdp"), None),
        P("fsdp", None, None),
        P("fsdp", None, None),
    )
    return jax.shard_map(
        on_device, mesh=mesh, in_specs=in_specs, out_specs=out_specs, check_vma=False
    )
```

profile of v0, /device:TPU:0, one launch (start us, length us, event | category | flops | bytes accessed | tf_op | source)
XLA Modules:
  0.0 445.9 jit_solution(9239581407377566130)
XLA Ops:
  7.2 0.7 all-gather.3.cloned.1.call-update
  8.0 0.7 all-gather.5.cloned.1.call-update
  8.7 4.4 copy.23
  13.2 0.7 copy.25
  13.9 1.2 gather_fusion.2
  15.2 1.2 gather_fusion.1
  16.5 1.2 gather_fusion
  17.7 1.4 gather_fusion.3
  19.1 7.5 %convolution_convert_fusion.7 = bf16[128,256,128]{2,0,1:T(8,128)(2,1)} fusion(bf16[256,48,128]{2,1,0:T(8,128)(2,1)} %bitcast.50, s32[128]{0:T(128)S(1)} %copy-done.2), kind=kOutput, calls=%fused_computation.43 | convolution fusion | flops 406853632 | bytes 11534848 | tf_op jit(solution)/shard_map/sr,rnk->snk/dot_general | solution.py:40
  26.6 5.6 %convolution_convert_fusion.5 = bf16[128,256,128]{2,0,1:T(8,128)(2,1)} fusion(bf16[256,48,128]{2,1,0:T(8,128)(2,1)S(1)} %bitcast.48, s32[128]{0:T(128)S(1)} %copy-done.2), kind=kOutput, calls=%fused_computation.41 | convolution fusion | flops 406853632 | bytes 11534848 | tf_op jit(solution)/shard_map/sr,rnk->snk/dot_general | solution.py:40
  32.2 5.6 %convolution_convert_fusion.3 = bf16[128,256,128]{2,0,1:T(8,128)(2,1)} fusion(bf16[256,48,128]{2,1,0:T(8,128)(2,1)S(1)} %bitcast.51, s32[128]{0:T(128)S(1)} %gather_fusion.1), kind=kOutput, calls=%fused_computation.39 | convolution fusion | flops 406853632 | bytes 11534848 | tf_op jit(solution)/shard_map/sr,rnk->snk/dot_general | solution.py:40
  37.9 20.9 %all-gather.3.cloned.1.call-done = bf16[128,128,128]{2,1,0:T(8,128)(2,1)} async-done(((bf16[4,128,128]{2,1,0:T(8,128)(2,1)}), bf16[128,128,128]{2,1,0:T(8,128)(2,1)}) %all-gather.3.cloned.1.call-update) | async-done | bytes 4194320 | tf_op jit(solution)/shard_map/all_gather | solution.py:71
  58.7 18.8 %fusion.27 = f32[128,256,128]{2,1,0:T(8,128)} fusion(bf16[128,256,128]{2,0,1:T(8,128)(2,1)} %convolution_convert_fusion.7, bf16[128,128,128]{2,1,0:T(8,128)(2,1)} %all-gather.3.cloned.1.call-done, bf16[128]{0:T(256)(128)(2,1)S(1)} %get-tuple-element.6), kind=kOutput, calls=%fused_computation.34 | convolution fusion | flops 1075838976 | bytes 29360384 | tf_op jit(solution)/shard_map/snk,skj->snj/dot_general | solution.py:74
  77.6 30.3 %fusion.13 = f32[192,256,128]{2,0,1:T(8,128)} fusion(f32[128,256,128]{2,1,0:T(8,128)} %fusion.27, s32[128]{0:T(128)S(1)} %copy-done.4), kind=kOutput, calls=%fused_computation.20 | convolution fusion | flops 9663700992 | bytes 41943552 | tf_op jit(solution)/shard_map/sc,snj->cnj/dot_general | solution.py:47
  107.9 18.5 %fusion.23 = f32[128,256,128]{2,1,0:T(8,128)} fusion(bf16[128,256,128]{2,0,1:T(8,128)(2,1)} %convolution_convert_fusion.5, bf16[128,128,128]{2,1,0:T(8,128)(2,1)} %all-gather.5.cloned.1.call-done, bf16[128]{0:T(256)(128)(2,1)S(1)} %get-tuple-element.6), kind=kOutput, calls=%fused_computation.30 | convolution fusion | flops 1075838976 | bytes 29360384 | tf_op jit(solution)/shard_map/snj,skj->snk/dot_general | solution.py:85
  126.5 44.2 %fusion.6 = bf16[192,256,128]{2,0,1:T(8,128)(2,1)S(1)} fusion(f32[192,256,128]{2,0,1:T(8,128)} %fusion.13, f32[128,256,128]{2,1,0:T(8,128)} %fusion.23, s32[128]{0:T(128)S(1)} %copy-done.4), kind=kOutput, calls=%fused_computation.12 | convolution fusion | flops 9783238656 | bytes 54526464 | tf_op jit(solution)/shard_map/sc,snj->cnj/dot_general | solution.py:47
  170.7 4.6 %copy-done.5 = bf16[192,256,128]{2,0,1:T(8,128)(2,1)} copy-done((bf16[192,256,128]{2,0,1:T(8,128)(2,1)}, bf16[192,256,128]{2,0,1:T(8,128)(2,1)S(1)}, u32[]{:S(2)}) %copy-start.5) | copy-done | bytes 12582936
  175.3 5.6 %convolution_convert_fusion.2 = bf16[128,256,128]{2,0,1:T(8,128)(2,1)} fusion(bf16[192,256,128]{2,0,1:T(8,128)(2,1)S(1)} %fusion.6, s32[128]{0:T(128)S(1)} %gather_fusion.2), kind=kOutput, calls=%fused_computation.38 | convolution fusion | flops 1614831616 | bytes 20972032 | tf_op jit(solution)/shard_map/sr,rnk->snk/dot_general | solution.py:40
  180.9 23.2 %broadcast_multiply_fusion.1 = f32[128,128,128]{2,1,0:T(8,128)} fusion(f32[128]{0:T(128)S(1)} %convert_element_type.86, bf16[128,256,128]{2,0,1:T(8,128)(2,1)} %convolution_convert_fusion.2, bf16[128,256,128]{2,0,1:T(8,128)(2,1)} %convolution_convert_fusion.3), kind=kOutput, calls=%fused_computation.45 | convolution fusion | flops 1075838976 | bytes 25166336 | tf_op jit(solution)/shard_map/snk,snj->skj/dot_general | solution.py:105
  204.2 5.6 %convolution_convert_fusion = bf16[128,256,128]{2,0,1:T(8,128)(2,1)} fusion(bf16[256,48,128]{2,1,0:T(8,128)(2,1)S(1)} %bitcast.49, s32[128]{0:T(128)S(1)} %gather_fusion.1), kind=kOutput, calls=%fused_computation.36 | convolution fusion | flops 406853632 | bytes 11534848 | tf_op jit(solution)/shard_map/sr,rnk->snk/dot_general | solution.py:40
  209.8 17.1 %convolution_convert_fusion.1 = bf16[128,256,128]{2,0,1:T(8,128)(2,1)} fusion(s32[128]{0:T(128)S(1)} %gather_fusion.2, f32[192,256,128]{2,0,1:T(8,128)} %fusion.13), kind=kOutput, calls=%fused_computation.37 | convolution fusion | flops 1671454720 | bytes 33554944 | tf_op jit(solution)/shard_map/sr,rnk->snk/dot_general | solution.py:40
  226.9 23.8 %broadcast_multiply_fusion = f32[128,128,128]{2,1,0:T(8,128)} fusion(f32[128]{0:T(128)S(1)} %convert_element_type.86, bf16[128,256,128]{2,0,1:T(8,128)(2,1)} %convolution_convert_fusion, bf16[128,256,128]{2,0,1:T(8,128)(2,1)} %convolution_convert_fusion.1), kind=kOutput, calls=%fused_computation.44 | convolution fusion | flops 1075838976 | bytes 25166336 | tf_op jit(solution)/shard_map/snk,snj->skj/dot_general | solution.py:115
  250.8 11.0 %convolution_convert_fusion.4 = bf16[128,256,128]{2,0,1:T(8,128)(2,1)} fusion(bf16[192,256,128]{2,0,1:T(8,128)(2,1)} %copy-done.5, s32[128]{0:T(128)S(1)} %copy-done.4), kind=kOutput, calls=%fused_computation.40 | convolution fusion | flops 1614831616 | bytes 20972032 | tf_op jit(solution)/shard_map/sr,rnk->snk/dot_general | solution.py:40
  261.8 18.8 %fusion.21 = f32[128,256,128]{2,1,0:T(8,128)} fusion(bf16[128,256,128]{2,0,1:T(8,128)(2,1)} %convolution_convert_fusion.4, bf16[128,128,128]{2,1,0:T(8,128)(2,1)} %all-gather.3.cloned.1.call-done, bf16[128]{0:T(256)(128)(2,1)S(1)} %get-tuple-element.6), kind=kOutput, calls=%fused_computation.28 | convolution fusion | flops 1075838976 | bytes 29360384 | tf_op jit(solution)/shard_map/snj,skj->snk/dot_general | solution.py:92
  280.6 21.6 %fusion.48 = bf16[48,256,128]{2,0,1:T(8,128)(2,1)S(1)} fusion(f32[128,256,128]{2,1,0:T(8,128)} %fusion.21, s32[128]{0:T(128)S(1)} %copy-done.3), kind=kOutput, calls=%fused_computation.57 | convolution fusion | flops 2417498112 | bytes 19923456 | tf_op jit(solution)/shard_map/sc,snj->cnj/dot_general | solution.py:47
  302.2 16.6 %convolution_convert_fusion.6 = bf16[128,256,128]{2,0,1:T(8,128)(2,1)} fusion(s32[128]{0:T(128)S(1)} %copy-done.4, f32[192,256,128]{2,0,1:T(8,128)} %fusion.13), kind=kOutput, calls=%fused_computation.42 | convolution fusion | flops 1671454720 | bytes 33554944 | tf_op jit(solution)/shard_map/sr,rnk->snk/dot_general | solution.py:40
  318.9 19.8 %fusion.25 = f32[128,256,128]{2,1,0:T(8,128)} fusion(bf16[128,256,128]{2,0,1:T(8,128)(2,1)} %convolution_convert_fusion.6, bf16[128,128,128]{2,1,0:T(8,128)(2,1)} %all-gather.5.cloned.1.call-done, bf16[128]{0:T(256)(128)(2,1)S(1)} %get-tuple-element.6), kind=kOutput, calls=%fused_computation.32 | convolution fusion | flops 1075838976 | bytes 29360384 | tf_op jit(solution)/shard_map/snk,skj->snj/dot_general | solution.py:84
  338.7 22.4 %fusion.45 = bf16[48,256,128]{2,0,1:T(8,128)(2,1)} fusion(f32[128,256,128]{2,1,0:T(8,128)} %fusion.25, s32[128]{0:T(128)S(1)} %copy-done.3), kind=kOutput, calls=%fused_computation.56 | convolution fusion | flops 2417498112 | bytes 19923456 | tf_op jit(solution)/shard_map/sc,snj->cnj/dot_general | solution.py:47
  361.1 31.2 %reduce-scatter.5.cloned.1.call-done = f32[4,128,128]{2,1,0:T(8,128)} async-done(((f32[128,128,128]{2,1,0:T(8,128)}), f32[4,128,128]{2,1,0:T(8,128)}) %reduce-scatter.5.cloned.1.call-update) | async-done | bytes 262160 | tf_op jit(solution)/shard_map/reduce_scatter | solution.py:114
  392.3 6.1 %copy_bitcast_fusion = (bf16[256,6144]{1,0:T(8,128)(2,1)}, bf16[256,6144]{1,0:T(8,128)(2,1)}) fusion(bf16[32,8,48,128]{3,2,1,0:T(8,128)(2,1)S(1)} %bitcast.52, bf16[32,8,48,128]{3,2,1,0:T(8,128)(2,1)} %bitcast.53), kind=kLoop, calls=%fused_computation.50 | loop fusion | bytes 12582912 | tf_op jit(solution)/shard_map/reshape | solution.py:31
  398.4 38.9 %all-reduce.3.cloned.1.call-done = (f32[4,128,128]{2,1,0:T(8,128)}, f32[4,128,128]{2,1,0:T(8,128)}) async-done(((f32[4,128,128]{2,1,0:T(8,128)}, f32[4,128,128]{2,1,0:T(8,128)}), (f32[4,128,128]{2,1,0:T(8,128)}, f32[4,128,128]{2,1,0:T(8,128)})) %all-reduce.3.cloned.1.call-update) | async-done | bytes 524304 | tf_op jit(solution)/shard_map/psum | solution.py:120
  437.3 1.9 broadcast_multiply_fusion.2
  (31 shorter events, 0.3 us)
Async XLA Ops:
  7.2 9.3 %copy-start = (s32[32]{0:T(128)S(1)}, s32[32]{0:T(128)}, u32[]{:S(2)}) copy-start(s32[32]{0:T(128)} %param.13) | copy-start | bytes 388
  7.2 6.8 %copy-start.4 = (s32[128]{0:T(128)S(1)}, s32[128]{0:T(128)}, u32[]{:S(2)}) copy-start(s32[128]{0:T(128)} %param.12) | copy-start | bytes 1540
  7.2 8.0 %copy-start.2 = (s32[128]{0:T(128)S(1)}, s32[128]{0:T(128)}, u32[]{:S(2)}) copy-start(s32[128]{0:T(128)} %param.11) | copy-start | bytes 1540
  7.2 51.5 %all-gather.3.cloned.1.call-start = ((), (), s32[]{:S(2)}) async-start(), calls=%async_computation.2 | async-start | bytes 4325376 | tf_op jit(solution)/shard_map/all_gather | solution.py:71
  7.9 100.0 %all-gather.5.cloned.1.call-start = ((), (), s32[]{:S(2)}) async-start(), calls=%async_computation.3 | async-start | bytes 4325376 | tf_op jit(solution)/shard_map/all_gather | solution.py:81
  8.7 352.4 %reduce-scatter.3.cloned.1.call-start = ((), (), s32[]{:S(2)}) async-start(), calls=%async_computation.4 | async-start | bytes 8650752 | tf_op jit(solution)/shard_map/reduce_scatter | solution.py:104
  8.7 4.4 copy-start.7
  26.6 5.6 %copy-start.6 = (bf16[32,8,48,128]{3,2,1,0:T(8,128)(2,1)S(1)}, bf16[32,8,48,128]{3,2,1,0:T(8,128)(2,1)}, u32[]{:S(2)}) copy-start(bf16[32,8,48,128]{3,2,1,0:T(8,128)(2,1)} %copy.23) | copy-start | bytes 9437188
  170.7 4.6 %copy-start.5 = (bf16[192,256,128]{2,0,1:T(8,128)(2,1)}, bf16[192,256,128]{2,0,1:T(8,128)(2,1)S(1)}, u32[]{:S(2)}) copy-start(bf16[192,256,128]{2,0,1:T(8,128)(2,1)S(1)} %fusion.6) | copy-start | bytes 37748740
  204.1 188.2 %reduce-scatter.5.cloned.1.call-start = ((), (), s32[]{:S(2)}) async-start(), calls=%async_computation.5 | async-start | bytes 8650752 | tf_op jit(solution)/shard_map/reduce_scatter | solution.py:114
  250.7 186.5 %all-reduce.3.cloned.1.call-start = ((), (), s32[]{:S(2)}) async-start(), calls=%async_computation.6 | async-start | bytes 1048576 | tf_op jit(solution)/shard_map/psum | solution.py:120
  261.8 18.8 %copy-start.3 = (s32[128]{0:T(128)S(1)}, s32[128]{0:T(128)}, u32[]{:S(2)}) copy-start(s32[128]{0:T(128)} %param.11) | copy-start | bytes 1540
  338.7 100.4 %copy-start.1 = (s32[32]{0:T(128)S(1)}, s32[32]{0:T(128)}, u32[]{:S(2)}) copy-start(s32[32]{0:T(128)} %param.13) | copy-start | bytes 388
Sparse Core Ops, SparseCore 0:
  10.3 48.3 all-gather.2
  61.0 45.3 all-gather.4
  204.2 92.0 reduce-scatter.2
  300.3 91.9 reduce-scatter.4
  394.5 42.6 all-reduce.2
where the time goes:
time: 449 us; the launch traced here: 446 us
  matrix products  316 us (70%)
  waiting for transfers between devices  92.4 us (21%)
  local copies, waits for them, and re-layouts  21 us (5%)
  between operations  14.2 us (3%)
    dot_general x4, matrix products, spread_blocks(): jnp.einsum('sc,snj->cnj', table, contrib, preferred_element_type=jnp.floa...  119 us
    dot_general x8, matrix products, pick_blocks(): jnp.einsum('sr,rnk->snk', table, blocks, preferred_element_type=jnp.float32)  74.6 us
    psum x1, waiting for transfers between devices, on_device(): up_grad, down_grad = lax.psum((up_local, down_local), 'dp')  38.9 us
    reduce_scatter x1, waiting for transfers between devices, on_device(): lax.psum_scatter(jnp.einsum('snk,snj->skj', h_pick, dy_pick, preferred_el...  31.2 us
    dot_general x1, matrix products, on_device(): jnp.einsum('snk,snj->skj', h_pick, dy_pick, preferred_element_type=jnp.fl...  23.8 us
    dot_general x1, matrix products, on_device(): jnp.einsum('snk,snj->skj', x_pick, p_pick, preferred_element_type=jnp.flo...  23.2 us
    all_gather x1, waiting for transfers between devices, on_device(): up_whole = lax.all_gather(up_weight_blocks, 'fsdp', axis=0, tiled=True)  20.9 us
    dot_general x1, matrix products, on_device(): jnp.einsum('snk,skj->snj', h_pick, weights, preferred_element_type=jnp.fl...  19.8 us
  transfers between devices with their start and end apart: 5, of which 3 were waited for; matrix products, arithmetic and copies ran while one was open for 54% of the time, Pallas kernels for 0%

commit v1 on v0

--- a/solution.py
+++ b/solution.py
@@ -68,7 +68,9 @@
     def slot_info():
         return (block_rows, block_cols, live_mask.astype(jnp.bfloat16)[:, None, None])
 
-    up_whole = lax.all_gather(up_weight_blocks, "fsdp", axis=0, tiled=True)
+    up_whole = jnp.concatenate(
+        lax.all_to_all(jnp.stack([up_weight_blocks] * lax.axis_size("fsdp")), "fsdp", 0, 0), axis=0
+    )
     row_ids, col_ids, keep_mask = slot_info()
     picked = pick_blocks(x_blocks, row_ids)
     contrib = jnp.einsum(

time: 449 us -> 444 us (0.989)
  waiting for transfers between devices: 92.4 us -> 69.5 us
  local copies, waits for them, and re-layouts: 21 us -> 28.7 us
  starting transfers between devices: 0.2 us -> 7.69 us
    reduce_scatter x1, waiting for transfers between devices: 31.2 us -> 0.01 us  [on_device(): lax.psum_scatter(jnp.einsum('snk,snj->skj', h_pick, dy_pick, preferred_el...]
    all_to_all x0 -> x1, waiting for transfers between devices: none -> 29.6 us  [on_device(): lax.all_to_all(jnp.stack([up_weight_blocks] * lax.axis_size('fsdp')), 'fs...]
    all_gather x1 -> x0, waiting for transfers between devices: 20.9 us -> none  [on_device(): up_whole = lax.all_gather(up_weight_blocks, 'fsdp', axis=0, tiled=True)]
    all_to_all x0 -> x1, starting transfers between devices: none -> 7.53 us  [on_device(): lax.all_to_all(jnp.stack([up_weight_blocks] * lax.axis_size('fsdp')), 'fs...]
    unnamed x18 -> x20, local copies, waits for them, and re-layouts: 9.8 us -> 13.3 us
  transfers between devices with their start and end apart: 5 -> 5, of which waited for: 3 -> 2; matrix products, arithmetic and copies ran while one was open for 54% -> 76% of each run, Pallas kernels for 0% -> 0%
where the time goes in v1:
time: 444 us; the launch traced here: 440 us
  matrix products  316 us (71%)
  waiting for transfers between devices  69.5 us (16%)
  local copies, waits for them, and re-layouts  28.7 us (6%)
  between operations  14.2 us (3%)
  starting transfers between devices  7.69 us (2%)
    dot_general x4, matrix products, spread_blocks(): jnp.einsum('sc,snj->cnj', table, contrib, preferred_element_type=jnp.floa...  120 us
    dot_general x8, matrix products, pick_blocks(): jnp.einsum('sr,rnk->snk', table, blocks, preferred_element_type=jnp.float32)  74.8 us
    psum x1, waiting for transfers between devices, on_device(): up_grad, down_grad = lax.psum((up_local, down_local), 'dp')  39.1 us
    all_to_all x1, waiting for transfers between devices, on_device(): lax.all_to_all(jnp.stack([up_weight_blocks] * lax.axis_size('fsdp')), 'fs...  29.6 us
    dot_general x1, matrix products, on_device(): jnp.einsum('snk,snj->skj', x_pick, p_pick, preferred_element_type=jnp.flo...  23.1 us
    dot_general x1, matrix products, on_device(): jnp.einsum('snk,snj->skj', h_pick, dy_pick, preferred_element_type=jnp.fl...  23 us
    dot_general x1, matrix products, on_device(): jnp.einsum('snj,skj->snk', dy_pick, weights, preferred_element_type=jnp.f...  20.3 us
    dot_general x1, matrix products, on_device(): jnp.einsum('snj,skj->snk', picked, up_whole * keep_mask, preferred_elemen...  19.1 us
  transfers between devices with their start and end apart: 5, of which 2 were waited for; matrix products, arithmetic and copies ran while one was open for 76% of the time, Pallas kernels for 0%

profile of v1, /device:TPU:0, one launch (start us, length us, event | category | flops | bytes accessed | tf_op | source)
XLA Modules:
  0.0 440.1 jit_solution(901417682188429765)
XLA Ops:
  7.2 3.9 stack.2
  11.1 7.5 %all-to-all-start = ((bf16[32,4,128,128]{3,2,1,0:T(8,128)(2,1)}), bf16[32,4,128,128]{3,2,1,0:T(8,128)(2,1)}, u32[]{:S(2)}, u32[]{:S(2)}) async-start(bf16[32,4,128,128]{3,2,1,0:T(8,128)(2,1)} %stack.2), calls=%async_computation | async-start | bytes 8388608 | tf_op jit(solution)/shard_map/all_to_all | solution.py:72
  19.4 2.6 copy.23
  22.1 4.3 copy.25
  26.4 1.2 gather_fusion.2
  28.9 1.2 gather_fusion
  30.1 1.7 gather_fusion.3
  31.9 5.6 %convolution_convert_fusion.7 = bf16[128,256,128]{2,0,1:T(8,128)(2,1)} fusion(bf16[256,48,128]{2,1,0:T(8,128)(2,1)S(1)} %bitcast.52, s32[128]{0:T(128)S(1)} %copy-done.2), kind=kOutput, calls=%fused_computation.43 | convolution fusion | flops 406853632 | bytes 11534848 | tf_op jit(solution)/shard_map/sr,rnk->snk/dot_general | solution.py:40
  37.5 5.6 %convolution_convert_fusion = bf16[128,256,128]{2,0,1:T(8,128)(2,1)} fusion(bf16[256,48,128]{2,1,0:T(8,128)(2,1)S(1)} %bitcast.55, s32[128]{0:T(128)S(1)} %gather_fusion.1), kind=kOutput, calls=%fused_computation.36 | convolution fusion | flops 406853632 | bytes 11534848 | tf_op jit(solution)/shard_map/sr,rnk->snk/dot_general | solution.py:40
  43.1 29.6 %all-to-all-done = bf16[32,4,128,128]{3,2,1,0:T(8,128)(2,1)} async-done(((bf16[32,4,128,128]{3,2,1,0:T(8,128)(2,1)}), bf16[32,4,128,128]{3,2,1,0:T(8,128)(2,1)}, u32[]{:S(2)}, u32[]{:S(2)}) %all-to-all-start) | async-done | bytes 4194336 | tf_op jit(solution)/shard_map/all_to_all | solution.py:72
  72.8 2.5 bitcast_multiply_fusion
  75.3 1.9 copy-done.5
  77.2 17.9 %fusion.27 = f32[128,256,128]{2,1,0:T(8,128)} fusion(bf16[128,128,128]{2,1,0:T(8,128)(2,1)S(1)} %bitcast_multiply_fusion, bf16[128,256,128]{2,0,1:T(8,128)(2,1)} %convolution_convert_fusion.7), kind=kOutput, calls=%fused_computation.34 | convolution fusion | flops 1073741824 | bytes 29360128 | tf_op jit(solution)/shard_map/snk,skj->snj/dot_general | solution.py:76
  95.1 29.9 %fusion.13 = f32[192,256,128]{2,0,1:T(8,128)} fusion(f32[128,256,128]{2,1,0:T(8,128)} %fusion.27, s32[128]{0:T(128)S(1)} %copy-done.3), kind=kOutput, calls=%fused_computation.20 | convolution fusion | flops 9663700992 | bytes 41943552 | tf_op jit(solution)/shard_map/sc,snj->cnj/dot_general | solution.py:47
  125.1 16.9 %convolution_convert_fusion.1 = bf16[128,256,128]{2,0,1:T(8,128)(2,1)} fusion(s32[128]{0:T(128)S(1)} %gather_fusion.2, f32[192,256,128]{2,0,1:T(8,128)} %fusion.13), kind=kOutput, calls=%fused_computation.37 | convolution fusion | flops 1671454720 | bytes 33554944 | tf_op jit(solution)/shard_map/sr,rnk->snk/dot_general | solution.py:40
  142.0 23.0 %broadcast_multiply_fusion = f32[128,128,128]{2,1,0:T(8,128)} fusion(f32[128]{0:T(128)S(1)} %convert_element_type.86, bf16[128,256,128]{2,0,1:T(8,128)(2,1)} %convolution_convert_fusion, bf16[128,256,128]{2,0,1:T(8,128)(2,1)} %convolution_convert_fusion.1), kind=kOutput, calls=%fused_computation.45 | convolution fusion | flops 1075838976 | bytes 25166336 | tf_op jit(solution)/shard_map/snk,snj->skj/dot_general | solution.py:117
  165.0 7.5 %convolution_convert_fusion.5 = bf16[128,256,128]{2,0,1:T(8,128)(2,1)} fusion(bf16[256,48,128]{2,1,0:T(8,128)(2,1)} %bitcast.54, s32[128]{0:T(128)S(1)} %copy-done.2), kind=kOutput, calls=%fused_computation.41 | convolution fusion | flops 406853632 | bytes 11534848 | tf_op jit(solution)/shard_map/sr,rnk->snk/dot_general | solution.py:40
  172.6 5.6 %convolution_convert_fusion.3 = bf16[128,256,128]{2,0,1:T(8,128)(2,1)} fusion(bf16[256,48,128]{2,1,0:T(8,128)(2,1)S(1)} %bitcast.53, s32[128]{0:T(128)S(1)} %gather_fusion.1), kind=kOutput, calls=%fused_computation.39 | convolution fusion | flops 406853632 | bytes 11534848 | tf_op jit(solution)/shard_map/sr,rnk->snk/dot_general | solution.py:40
  178.2 20.3 %fusion.23 = f32[128,256,128]{2,1,0:T(8,128)} fusion(bf16[128,256,128]{2,0,1:T(8,128)(2,1)} %convolution_convert_fusion.5, bf16[128,128,128]{2,1,0:T(8,128)(2,1)} %all-gather.2.cloned.1.call-done, bf16[128]{0:T(256)(128)(2,1)S(1)} %get-tuple-element.6), kind=kOutput, calls=%fused_computation.30 | convolution fusion | flops 1075838976 | bytes 29360384 | tf_op jit(solution)/shard_map/snj,skj->snk/dot_general | solution.py:87
  198.5 44.5 %fusion.6 = bf16[192,256,128]{2,0,1:T(8,128)(2,1)S(1)} fusion(f32[192,256,128]{2,0,1:T(8,128)} %fusion.13, f32[128,256,128]{2,1,0:T(8,128)} %fusion.23, s32[128]{0:T(128)S(1)} %copy-done.3), kind=kOutput, calls=%fused_computation.12 | convolution fusion | flops 9783238656 | bytes 54526464 | tf_op jit(solution)/shard_map/sc,snj->cnj/dot_general | solution.py:47
  243.0 4.5 %copy-done.4 = bf16[192,256,128]{2,0,1:T(8,128)(2,1)} copy-done((bf16[192,256,128]{2,0,1:T(8,128)(2,1)}, bf16[192,256,128]{2,0,1:T(8,128)(2,1)S(1)}, u32[]{:S(2)}) %copy-start.4) | copy-done | bytes 12582936
  247.5 5.7 %convolution_convert_fusion.2 = bf16[128,256,128]{2,0,1:T(8,128)(2,1)} fusion(bf16[192,256,128]{2,0,1:T(8,128)(2,1)S(1)} %fusion.6, s32[128]{0:T(128)S(1)} %gather_fusion.2), kind=kOutput, calls=%fused_computation.38 | convolution fusion | flops 1614831616 | bytes 20972032 | tf_op jit(solution)/shard_map/sr,rnk->snk/dot_general | solution.py:40
  253.2 23.1 %broadcast_multiply_fusion.1 = f32[128,128,128]{2,1,0:T(8,128)} fusion(f32[128]{0:T(128)S(1)} %convert_element_type.86, bf16[128,256,128]{2,0,1:T(8,128)(2,1)} %convolution_convert_fusion.2, bf16[128,256,128]{2,0,1:T(8,128)(2,1)} %convolution_convert_fusion.3), kind=kOutput, calls=%fused_computation.46 | convolution fusion | flops 1075838976 | bytes 25166336 | tf_op jit(solution)/shard_map/snk,snj->skj/dot_general | solution.py:107
  276.5 16.9 %convolution_convert_fusion.6 = bf16[128,256,128]{2,0,1:T(8,128)(2,1)} fusion(s32[128]{0:T(128)S(1)} %copy-done.3, f32[192,256,128]{2,0,1:T(8,128)} %fusion.13), kind=kOutput, calls=%fused_computation.42 | convolution fusion | flops 1671454720 | bytes 33554944 | tf_op jit(solution)/shard_map/sr,rnk->snk/dot_general | solution.py:40
  293.4 10.9 %convolution_convert_fusion.4 = bf16[128,256,128]{2,0,1:T(8,128)(2,1)} fusion(bf16[192,256,128]{2,0,1:T(8,128)(2,1)} %copy-done.4, s32[128]{0:T(128)S(1)} %copy-done.3), kind=kOutput, calls=%fused_computation.40 | convolution fusion | flops 1614831616 | bytes 20972032 | tf_op jit(solution)/shard_map/sr,rnk->snk/dot_general | solution.py:40
  304.2 19.1 %fusion.21 = f32[128,256,128]{2,1,0:T(8,128)} fusion(bf16[128,128,128]{2,1,0:T(8,128)(2,1)} %copy-done.5, bf16[128,256,128]{2,0,1:T(8,128)(2,1)} %convolution_convert_fusion.4), kind=kOutput, calls=%fused_computation.28 | convolution fusion | flops 1073741824 | bytes 29360128 | tf_op jit(solution)/shard_map/snj,skj->snk/dot_general | solution.py:94
  323.3 22.7 %fusion.46 = bf16[48,256,128]{2,0,1:T(8,128)(2,1)} fusion(f32[128,256,128]{2,1,0:T(8,128)} %fusion.21, s32[128]{0:T(128)S(1)} %copy-done.2), kind=kOutput, calls=%fused_computation.56 | convolution fusion | flops 2417498112 | bytes 19923456 | tf_op jit(solution)/shard_map/sc,snj->cnj/dot_general | solution.py:47
  346.0 17.6 %fusion.25 = f32[128,256,128]{2,1,0:T(8,128)} fusion(bf16[128,256,128]{2,0,1:T(8,128)(2,1)} %convolution_convert_fusion.6, bf16[128,128,128]{2,1,0:T(8,128)(2,1)S(1)} %copy-done.7, bf16[128]{0:T(256)(128)(2,1)S(1)} %get-tuple-element.6), kind=kOutput, calls=%fused_computation.32 | convolution fusion | flops 1075838976 | bytes 29360384 | tf_op jit(solution)/shard_map/snk,skj->snj/dot_general | solution.py:86
  363.6 22.5 %fusion.43 = bf16[48,256,128]{2,0,1:T(8,128)(2,1)} fusion(f32[128,256,128]{2,1,0:T(8,128)} %fusion.25, s32[128]{0:T(128)S(1)} %copy-done.2), kind=kOutput, calls=%fused_computation.55 | convolution fusion | flops 2417498112 | bytes 19923456 | tf_op jit(solution)/shard_map/sc,snj->cnj/dot_general | solution.py:47
  386.2 6.1 %copy_bitcast_fusion = (bf16[256,6144]{1,0:T(8,128)(2,1)}, bf16[256,6144]{1,0:T(8,128)(2,1)}) fusion(bf16[32,8,48,128]{3,2,1,0:T(8,128)(2,1)S(1)} %bitcast.56, bf16[32,8,48,128]{3,2,1,0:T(8,128)(2,1)} %bitcast.57), kind=kLoop, calls=%fused_computation.49 | loop fusion | bytes 12582912 | tf_op jit(solution)/shard_map/reshape | solution.py:31
  392.3 39.1 %all-reduce.3.cloned.1.call-done = (f32[4,128,128]{2,1,0:T(8,128)}, f32[4,128,128]{2,1,0:T(8,128)}) async-done(((f32[4,128,128]{2,1,0:T(8,128)}, f32[4,128,128]{2,1,0:T(8,128)}), (f32[4,128,128]{2,1,0:T(8,128)}, f32[4,128,128]{2,1,0:T(8,128)})) %all-reduce.3.cloned.1.call-update) | async-done | bytes 524304 | tf_op jit(solution)/shard_map/psum | solution.py:122
  431.4 1.9 broadcast_multiply_fusion.2
  (34 shorter events, 2.2 us)
Async XLA Ops:
  7.2 21.7 %copy-start = (s32[32]{0:T(128)S(1)}, s32[32]{0:T(128)}, u32[]{:S(2)}) copy-start(s32[32]{0:T(128)} %param.13) | copy-start | bytes 388
  11.1 61.7 %all-to-all-start = ((bf16[32,4,128,128]{3,2,1,0:T(8,128)(2,1)}), bf16[32,4,128,128]{3,2,1,0:T(8,128)(2,1)}, u32[]{:S(2)}, u32[]{:S(2)}) async-start(bf16[32,4,128,128]{3,2,1,0:T(8,128)(2,1)} %stack.2), calls=%async_computation | async-start | bytes 8388608 | tf_op jit(solution)/shard_map/all_to_all | solution.py:72
  18.6 7.7 %copy-start.3 = (s32[128]{0:T(128)S(1)}, s32[128]{0:T(128)}, u32[]{:S(2)}) copy-start(s32[128]{0:T(128)} %param.12) | copy-start | bytes 1540
  18.6 9.0 %copy-start.2 = (s32[128]{0:T(128)S(1)}, s32[128]{0:T(128)}, u32[]{:S(2)}) copy-start(s32[128]{0:T(128)} %param.11) | copy-start | bytes 1540
  18.7 159.5 %all-gather.2.cloned.1.call-start = ((), (), s32[]{:S(2)}) async-start(), calls=%async_computation.3 | async-start | bytes 4325376 | tf_op jit(solution)/shard_map/all_gather | solution.py:83
  19.4 366.8 %reduce-scatter.5.cloned.1.call-start = ((), (), s32[]{:S(2)}) async-start(), calls=%async_computation.5 | async-start | bytes 8650752 | tf_op jit(solution)/shard_map/reduce_scatter | solution.py:116
  31.8 5.7 %copy-start.6 = (bf16[32,8,48,128]{3,2,1,0:T(8,128)(2,1)S(1)}, bf16[32,8,48,128]{3,2,1,0:T(8,128)(2,1)}, u32[]{:S(2)}) copy-start(bf16[32,8,48,128]{3,2,1,0:T(8,128)(2,1)} %copy.25) | copy-start | bytes 9437188
  75.3 1.9 copy-start.5
  165.0 221.2 %reduce-scatter.3.cloned.1.call-start = ((), (), s32[]{:S(2)}) async-start(), calls=%async_computation.4 | async-start | bytes 8650752 | tf_op jit(solution)/shard_map/reduce_scatter | solution.py:106
  243.0 4.5 %copy-start.4 = (bf16[192,256,128]{2,0,1:T(8,128)(2,1)}, bf16[192,256,128]{2,0,1:T(8,128)(2,1)S(1)}, u32[]{:S(2)}) copy-start(bf16[192,256,128]{2,0,1:T(8,128)(2,1)S(1)} %fusion.6) | copy-start | bytes 37748740
  276.4 155.0 %all-reduce.3.cloned.1.call-start = ((), (), s32[]{:S(2)}) async-start(), calls=%async_computation.6 | async-start | bytes 1048576 | tf_op jit(solution)/shard_map/psum | solution.py:122
  323.3 22.7 %copy-start.7 = (bf16[128,128,128]{2,1,0:T(8,128)(2,1)S(1)}, bf16[128,128,128]{2,1,0:T(8,128)(2,1)}, u32[]{:S(2)}) copy-start(bf16[128,128,128]{2,1,0:T(8,128)(2,1)} %all-gather.2.cloned.1.call-done) | copy-start | bytes 12582916
  363.6 22.6 %copy-start.8 = (bf16[48,256,128]{2,0,1:T(8,128)(2,1)S(1)}, bf16[48,256,128]{2,0,1:T(8,128)(2,1)}, u32[]{:S(2)}) copy-start(bf16[48,256,128]{2,0,1:T(8,128)(2,1)} %fusion.46) | copy-start | bytes 9437188
  363.6 69.7 %copy-start.1 = (s32[32]{0:T(128)S(1)}, s32[32]{0:T(128)}, u32[]{:S(2)}) copy-start(s32[32]{0:T(128)} %param.13) | copy-start | bytes 388
Sparse Core Ops, SparseCore 0:
  21.8 72.3 all-gather.1
  165.1 94.1 reduce-scatter.4
  276.5 94.2 reduce-scatter.2
  386.3 45.0 all-reduce.2
